TPU v7x, 32 devices: a whole 2x2x4 slice. The times are simulated.
32 devices in a mesh: phase: 2 (over x), expert: 4 (over y, core), tensor: 4 (over z).
Axes of the slice: x: 2, y: 2, z: 4, core: 2. Of those that a mesh axis runs over, the one named last changes fastest.
Arguments:
- forward_routes: int32 [2, 256, 6], P('phase', 'expert'), may hold values from 0 to 11, all different within a row; in each aligned block of 64 rows (0 to 63, 64 to 127, ..., all dimensions but the last counted through in order) at most 43 rows name the same one
- forward_gates: float32 [2, 256, 6], P('phase', 'expert'), may hold values from 0.05 to 1
- hidden_rows: bfloat16 [2, 12, 4, 43, 1024], P('phase', 'expert', None, None, 'tensor'), may hold values from -6 to 6
- down_weight: bfloat16 [2, 12, 1024, 2560], P('phase', 'expert', 'tensor'), may hold values from -0.1875 to 0.1875
- shared_hidden: bfloat16 [2, 256, 1536], P('phase', 'expert', 'tensor'), may hold values from -6 to 6
- shared_weight: bfloat16 [2, 1536, 2560], P('phase', 'tensor', 'expert'), may hold values from -0.15625 to 0.15625
- backward_routes: int32 [2, 256, 6], P('phase', 'expert'), may hold values from 0 to 11, all different within a row; in each aligned block of 64 rows (0 to 63, 64 to 127, ..., all dimensions but the last counted through in order) at most 43 rows name the same one
- backward_gates: float32 [2, 256, 6], P('phase', 'expert'), may hold values from 0.05 to 1
- cotangent: bfloat16 [2, 256, 2560], P('phase', 'expert', 'tensor'), may hold values from -6 to 6
Outputs:
- forward_next: bfloat16 [2, 256, 2560], P('phase', 'expert', 'tensor')
- hidden_grad: bfloat16 [2, 12, 4, 43, 1024], P('phase', 'expert', None, None, 'tensor')
- shared_grad: bfloat16 [2, 256, 1536], P('phase', 'expert', 'tensor')
Inputs may be any that keep to these rules, and one draw needn't show every extreme that they name: `forward_routes`: each token names 6 different experts. The tokens of one token group (the 64 rows of one device) name any one expert 43 times at most, and some group reaches that. `backward_routes`: as for forward_routes.
All inputs are finite; a program needn't handle non-finite values.
Results may differ from a plain program's by a relative error of at most 0.0049.
Values may be sent and summed in bfloat16 or wider, within the bound.
A program may use at most 64 MiB of HBM per device.

v0:
```python
import jax
import jax.numpy as jnp
from jax import lax
from jax.sharding import PartitionSpec as P


def shifted(value, axis, steps):
    count = lax.axis_size(axis)
    pairs = [(source, (source + steps) % count) for source in range(count)]
    return lax.ppermute(value, axis, pairs)


def slot_numbers(routes, experts):
    numbers = jnp.arange(experts, dtype=jnp.int32)
    onehot = (routes[:, :, None] == numbers[None, None, :]).astype(jnp.int32)
    per_token = jnp.sum(onehot, axis=1)
    before = jnp.cumsum(per_token, axis=0) - per_token
    return jnp.sum(onehot * before[:, None, :], axis=2)


def row_positions(routes, experts_here, groups, capacity):
    slot_index = slot_numbers(routes, experts_here * groups)
    holder = routes // experts_here
    within = routes - holder * experts_here
    return ((within * groups + holder) * capacity + slot_index).reshape(-1)


def place_rows(gates, values, positions, total_rows):
    scaled = (gates[:, :, None] * values[:, None, :].astype(jnp.float32)).astype(jnp.bfloat16)
    outgoing = jnp.zeros((total_rows, values.shape[1]), jnp.bfloat16)
    return outgoing.at[positions].set(scaled.reshape(-1, values.shape[1]))


def on_device(
    forward_routes,
    forward_gates,
    hidden_rows,
    down_weight,
    shared_hidden,
    shared_weight,
    backward_routes,
    backward_gates,
    cotangent,
):
    experts_here = down_weight.shape[1]
    features = down_weight.shape[3]
    capacity = hidden_rows.shape[3]
    groups = lax.axis_size("expert")
    token_count = forward_routes.shape[1]
    top_count = forward_routes.shape[2]
    hidden = hidden_rows[0]
    weight = down_weight[0]
    local_shared = shared_hidden[0]
    shared_piece = shared_weight[0]
    shared_part = jnp.dot(
        local_shared,
        lax.all_gather(shared_piece, "expert", axis=1, tiled=True),
        preferred_element_type=jnp.float32,
    )
    fore_positions = row_positions(forward_routes[0], experts_here, groups, capacity)
    fore_gates = forward_gates[0]
    partial_value = jnp.einsum(
        "egmh,ehd->egmd", hidden, weight, preferred_element_type=jnp.float32
    ).astype(jnp.bfloat16)
    arrived = lax.all_to_all(partial_value, "expert", split_axis=1, concat_axis=1, tiled=True)
    picked = arrived.reshape(-1, features)[fore_positions].reshape(token_count, top_count, features)
    summand = shared_part + jnp.sum(picked.astype(jnp.float32) * fore_gates[:, :, None], axis=1)
    summed = lax.psum_scatter(summand, "tensor", scatter_dimension=1, tiled=True)
    layer_out = summed.astype(jnp.bfloat16)
    handed = shifted(layer_out, "phase", 1)
    cotangent_whole = lax.all_gather(cotangent[0], "tensor", axis=1, tiled=True)
    back_positions = row_positions(backward_routes[0], experts_here, groups, capacity)
    total_rows = experts_here * groups * capacity
    outgoing = place_rows(backward_gates[0], cotangent_whole, back_positions, total_rows)
    received = lax.all_to_all(
        outgoing.reshape(experts_here, groups, capacity, features),
        "expert",
        split_axis=1,
        concat_axis=1,
        tiled=True,
    )
    hidden_back = jnp.einsum(
        "egmd,ehd->egmh", received, weight, preferred_element_type=jnp.float32
    ).astype(jnp.bfloat16)
    shared_back = lax.dot_general(
        cotangent_whole,
        lax.all_gather(shared_piece, "expert", axis=1, tiled=True),
        (((1,), (1,)), ((), ())),
        preferred_element_type=jnp.float32,
    )
    return (handed[None], hidden_back[None], shared_back.astype(jnp.bfloat16)[None])


def solution(mesh):
    return jax.shard_map(
        on_device,
        mesh=mesh,
        in_specs=(
            P("phase", "expert", None),
            P("phase", "expert", None),
            P("phase", "expert", None, None, "tensor"),
            P("phase", "expert", "tensor", None),
            P("phase", "expert", "tensor"),
            P("phase", "tensor", "expert"),
            P("phase", "expert", None),
            P("phase", "expert", None),
            P("phase", "expert", "tensor"),
        ),
        out_specs=(
            P("phase", "expert", "tensor"),
            P("phase", "expert", None, None, "tensor"),
            P("phase", "expert", "tensor"),
        ),
        check_vma=False,
    )
```

profile of v0, /device:TPU:0, one launch (start us, length us, event | category | flops | bytes accessed | tf_op | source)
XLA Modules:
  0.0 125.8 jit_solution(11114866038983174019)
XLA Ops:
  7.2 0.0 all-gather.4.cloned.1.call-start
  7.2 0.7 all-gather.4.cloned.1.call-update
  7.9 3.2 %convolution_convert_fusion = bf16[3,4,43,2560]{3,2,1,0:T(8,128)(2,1)S(1)} fusion(bf16[1,3,256,2560]{3,2,1,0:T(8,128)(2,1)} %param.12, bf16[3,4,43,256]{3,1,2,0:T(4,128)(2,1)} %bitcast.42), kind=kOutput, calls=%fused_computation.3 | convolution fusion | flops 677652480 | bytes 6838272 | tf_op jit(solution)/shard_map/egmh,ehd->egmd/dot_general | solution.py:62
  11.1 1.8 %copy.38 = bf16[3,4,43,2560]{3,2,0,1:T(8,128)(2,1)} copy(bf16[3,4,43,2560]{3,2,1,0:T(8,128)(2,1)S(1)} %convolution_convert_fusion) | data formatting | bytes 5283840 | tf_op jit(solution)/shard_map/convert_element_type | solution.py:64
  12.8 4.4 %all-to-all-start = ((bf16[3,4,43,2560]{3,2,0,1:T(8,128)(2,1)}), bf16[3,4,43,2560]{3,2,0,1:T(8,128)(2,1)S(1)}, u32[]{:S(2)}, u32[]{:S(2)}) async-start(bf16[3,4,43,2560]{3,2,0,1:T(8,128)(2,1)} %copy.38), calls=%async_computation | async-start | bytes 5898240 | tf_op jit(solution)/shard_map/all_to_all | solution.py:65
  17.2 0.1 copy.46
  17.4 0.1 copy.47
  17.4 0.1 reduce_window_sum.18
  17.5 0.1 copy.49
  17.7 0.1 copy.50
  17.8 0.1 reduce_sum.55
  17.9 0.1 copy.51
  18.0 0.1 mul.123
  18.1 0.1 squeeze.26
  18.3 15.6 %all-gather.1 = bf16[1,64,2560]{2,1,0:T(8,128)(2,1)S(1)} all-gather(bf16[1,64,640]{2,1,0:T(8,128)(2,1)S(1)} %copy-done.2), channel_id=3, replica_groups=mesh['phase'=2,'expert'=4,'tensor'=4] {'tensor'}, dimensions={2}, use_global_device_ids=true | all-gather | bytes 409600 | tf_op jit(solution)/shard_map/all_gather | solution.py:71
  33.9 3.0 %mul.125 = f32[64,6,2560]{2,1,0:T(8,128)} broadcast(f32[64,2560]{1,0:T(8,128)S(1)} %bitcast_convert_fusion), dimensions={0,2} | broadcast | bytes 4587520 | tf_op jit(solution)/shard_map/mul | solution.py:29
  36.9 5.1 %mul.126 = f32[384,2560]{1,0:T(8,128)} reshape(f32[64,6,2560]{2,1,0:T(8,128)} %mul.125) | data formatting | bytes 7864320 | tf_op jit(solution)/shard_map/mul | solution.py:29
  42.0 6.8 %scatter_custom_fusion = bf16[516,2560]{1,0:T(8,128)(2,1)} fusion(s32[384]{0:T(512)S(1)} %fusion.30, f32[384,2560]{1,0:T(8,128)} %mul.126, f32[384]{0:T(512)S(1)} %mul.123, bf16[]{:T(256)} %constant.32.clone.1), kind=kCustom, calls=%fused_computation.10 | custom fusion | flops 1966080 | bytes 6576130 | tf_op jit(solution)/shard_map/scatter | solution.py:31
  48.9 3.6 %reshape.216 = bf16[3,4,43,2560]{3,2,1,0:T(8,128)(2,1)} reshape(bf16[516,2560]{1,0:T(8,128)(2,1)} %scatter_custom_fusion) | data formatting | bytes 5283840 | tf_op jit(solution)/shard_map/reshape | solution.py:76
  52.5 3.6 %copy.52 = bf16[3,4,43,2560]{3,2,0,1:T(8,128)(2,1)} copy(bf16[3,4,43,2560]{3,2,1,0:T(8,128)(2,1)} %reshape.216) | data formatting | bytes 5283840 | tf_op jit(solution)/shard_map/reshape | solution.py:76
  56.1 6.5 %all-to-all-done = bf16[3,4,43,2560]{3,2,0,1:T(8,128)(2,1)S(1)} async-done(((bf16[3,4,43,2560]{3,2,0,1:T(8,128)(2,1)}), bf16[3,4,43,2560]{3,2,0,1:T(8,128)(2,1)S(1)}, u32[]{:S(2)}, u32[]{:S(2)}) %all-to-all-start) | async-done | bytes 2641952 | tf_op jit(solution)/shard_map/all_to_all | solution.py:65
  62.6 4.7 %all-to-all-start.1 = ((bf16[3,4,43,2560]{3,2,0,1:T(8,128)(2,1)}), bf16[3,4,43,2560]{3,2,0,1:T(8,128)(2,1)}, u32[]{:S(2)}, u32[]{:S(2)}) async-start(bf16[3,4,43,2560]{3,2,0,1:T(8,128)(2,1)} %copy.52), calls=%async_computation.2 | async-start | bytes 5898240 | tf_op jit(solution)/shard_map/all_to_all | solution.py:75
  67.3 0.2 reduce-scatter.2.cloned.1.call-start
  67.6 0.1 copy.40
  67.7 0.1 copy.41
  67.8 0.1 reduce_window_sum.17
  67.9 0.1 copy.43
  68.0 0.1 copy.44
  68.1 0.1 reduce_sum.51
  68.2 0.1 copy.56
  68.3 0.1 squeeze.25
  68.5 1.8 %copy.39 = bf16[3,4,43,2560]{3,2,1,0:T(8,128)(2,1)} copy(bf16[3,4,43,2560]{3,2,0,1:T(8,128)(2,1)S(1)} %all-to-all-done) | data formatting | bytes 5283840 | tf_op jit(solution)/shard_map/all_to_all | solution.py:65
  70.4 2.4 %reshape.215 = bf16[516,2560]{1,0:T(8,128)(2,1)S(1)} reshape(bf16[3,4,43,2560]{3,2,1,0:T(8,128)(2,1)} %copy.39) | data formatting | bytes 5283840 | tf_op jit(solution)/shard_map/reshape | solution.py:66
  72.8 3.3 %gather_fusion = bf16[384,2560]{1,0:T(8,128)(2,1)} fusion(bf16[516,2560]{1,0:T(8,128)(2,1)S(1)} %reshape.215, s32[1024]{0:T(1024)S(1)} %pad_clamp_fusion), kind=kCustom, calls=%fused_computation | custom fusion | bytes 3933696 | tf_op jit(solution)/shard_map/gather | solution.py:66
  76.1 4.5 %reshape.217 = f32[64,6,2560]{2,1,0:T(8,128)} reshape(bf16[384,2560]{1,0:T(8,128)(2,1)} %gather_fusion) | data formatting | bytes 5898240 | tf_op jit(solution)/shard_map/convert_element_type | solution.py:67
  80.5 4.4 %multiply_reduce_fusion = f32[64,2560]{1,0:T(8,128)S(1)} fusion(f32[64,6,2560]{2,1,0:T(8,128)} %reshape.217, f32[64,6]{1,0:T(8,128)S(1)} %bitcast.43), kind=kLoop, calls=%fused_computation.2 | loop fusion | flops 1802240 | bytes 4589056 | tf_op jit(solution)/shard_map/reduce_sum | solution.py:67
  85.0 0.0 all-gather.4.cloned.1.call-done
  85.0 2.9 %convolution_add_fusion = f32[64,2560]{1,0:T(8,128)} fusion(f32[64,2560]{1,0:T(8,128)S(1)} %multiply_reduce_fusion, bf16[1,384,2560]{2,1,0:T(8,128)(2,1)} %all-gather.4.cloned.1.call-done, bf16[1,64,384]{2,1,0:T(8,128)(2,1)S(1)} %copy-done), kind=kOutput, calls=%fused_computation.8 | convolution fusion | flops 125992960 | bytes 3325952 | tf_op jit(solution)/shard_map/dot_general | solution.py:55
  87.8 0.0 reduce-scatter.2.cloned.1.call-update
  87.9 14.3 %all-to-all-done.1 = bf16[3,4,43,2560]{3,2,0,1:T(8,128)(2,1)} async-done(((bf16[3,4,43,2560]{3,2,0,1:T(8,128)(2,1)}), bf16[3,4,43,2560]{3,2,0,1:T(8,128)(2,1)}, u32[]{:S(2)}, u32[]{:S(2)}) %all-to-all-start.1) | async-done | bytes 2641952 | tf_op jit(solution)/shard_map/all_to_all | solution.py:75
  102.2 4.5 %fusion.15 = bf16[1,3,4,43,256]{4,3,2,1,0:T(8,128)(2,1)S(1)} fusion(bf16[1,3,256,2560]{3,2,1,0:T(8,128)(2,1)} %param.12, bf16[3,4,43,2560]{3,2,0,1:T(8,128)(2,1)} %all-to-all-done.1), kind=kOutput, calls=%fused_computation.17 | convolution fusion | flops 676463616 | bytes 6838272 | tf_op jit(solution)/shard_map/egmd,ehd->egmh/dot_general | solution.py:82
  106.7 0.8 copy.54
  107.5 5.3 %reduce-scatter.2.cloned.1.call-done = f32[64,640]{1,0:T(8,128)} async-done(((f32[64,2560]{1,0:T(8,128)}), f32[64,640]{1,0:T(8,128)}) %reduce-scatter.2.cloned.1.call-update) | async-done | bytes 163856 | tf_op jit(solution)/shard_map/reduce_scatter | solution.py:68
  112.8 0.9 convert_element_type.36
  113.8 1.5 %collective-permute-start = (bf16[64,640]{1,0:T(8,128)(2,1)S(1)}, bf16[64,640]{1,0:T(8,128)(2,1)S(1)}, u32[]{:S(2)}, u32[]{:S(2)}) collective-permute-start(bf16[64,640]{1,0:T(8,128)(2,1)S(1)} %convert_element_type.36), channel_id=1, source_target_pairs={{0,16},{16,0},{1,17},{17,1},{2,18},{18,2},{3,19},{19,3},{4,20},{20... | collective-permute-start | bytes 245768 | tf_op jit(solution)/shard_map/ppermute | solution.py:10
  115.3 1.4 %fusion.23 = bf16[1,64,384]{2,1,0:T(8,128)(2,1)} fusion(bf16[1,384,2560]{2,1,0:T(8,128)(2,1)S(1)} %copy-done.1, bf16[1,64,2560]{2,1,0:T(8,128)(2,1)S(1)} %all-gather.1), kind=kOutput, calls=%fused_computation.19 | convolution fusion | flops 125853696 | bytes 2342912 | tf_op jit(solution)/shard_map/dot_general | solution.py:85
  116.7 1.6 %collective-permute-done = bf16[64,640]{1,0:T(8,128)(2,1)S(1)} collective-permute-done((bf16[64,640]{1,0:T(8,128)(2,1)S(1)}, bf16[64,640]{1,0:T(8,128)(2,1)S(1)}, u32[]{:S(2)}, u32[]{:S(2)}) %collective-permute-start) | collective-permute-done | bytes 81952 | tf_op jit(solution)/shard_map/ppermute | solution.py:10
  118.3 0.6 copy.72
  (26 shorter events, 0.3 us)
Async XLA Ops:
  7.2 77.8 %copy-start = (bf16[1,64,384]{2,1,0:T(8,128)(2,1)S(1)}, bf16[1,64,384]{2,1,0:T(8,128)(2,1)}, u32[]{:S(2)}) copy-start(bf16[1,64,384]{2,1,0:T(8,128)(2,1)} %param.13) | copy-start | bytes 147460
  7.2 77.8 %all-gather.4.cloned.1.call-start = ((), (), s32[]{:S(2)}) async-start(), calls=%async_computation.4 | async-start | bytes 2457600 | tf_op jit(solution)/shard_map/all_gather | solution.py:57
  12.8 4.4 %copy-start.3 = (s32[1,64,6]{1,0,2:T(1,128)S(1)}, s32[1,64,6]{1,0,2:T(1,128)}, u32[]{:S(2)}) copy-start(s32[1,64,6]{1,0,2:T(1,128)} %param.15) | copy-start | bytes 4612
  12.8 5.1 %copy-start.5 = (f32[1,64,6]{1,0,2:T(1,128)S(1)}, f32[1,64,6]{1,0,2:T(1,128)}, u32[]{:S(2)}) copy-start(f32[1,64,6]{1,0,2:T(1,128)} %param.16) | copy-start | bytes 4612
  12.8 5.5 %copy-start.2 = (bf16[1,64,640]{2,1,0:T(8,128)(2,1)S(1)}, bf16[1,64,640]{2,1,0:T(8,128)(2,1)}, u32[]{:S(2)}) copy-start(bf16[1,64,640]{2,1,0:T(8,128)(2,1)} %param.17) | copy-start | bytes 245764
  12.8 49.8 %all-to-all-start = ((bf16[3,4,43,2560]{3,2,0,1:T(8,128)(2,1)}), bf16[3,4,43,2560]{3,2,0,1:T(8,128)(2,1)S(1)}, u32[]{:S(2)}, u32[]{:S(2)}) async-start(bf16[3,4,43,2560]{3,2,0,1:T(8,128)(2,1)} %copy.38), calls=%async_computation | async-start | bytes 5898240 | tf_op jit(solution)/shard_map/all_to_all | solution.py:65
  56.1 11.5 %copy-start.4 = (s32[1,64,6]{1,0,2:T(1,128)S(1)}, s32[1,64,6]{1,0,2:T(1,128)}, u32[]{:S(2)}) copy-start(s32[1,64,6]{1,0,2:T(1,128)} %param.9) | copy-start | bytes 4612
  56.1 12.1 %copy-start.6 = (f32[1,64,6]{1,0,2:T(1,128)S(1)}, f32[1,64,6]{1,0,2:T(1,128)}, u32[]{:S(2)}) copy-start(f32[1,64,6]{1,0,2:T(1,128)} %param.10) | copy-start | bytes 4612
  62.6 39.5 %all-to-all-start.1 = ((bf16[3,4,43,2560]{3,2,0,1:T(8,128)(2,1)}), bf16[3,4,43,2560]{3,2,0,1:T(8,128)(2,1)}, u32[]{:S(2)}, u32[]{:S(2)}) async-start(bf16[3,4,43,2560]{3,2,0,1:T(8,128)(2,1)} %copy.52), calls=%async_computation.2 | async-start | bytes 5898240 | tf_op jit(solution)/shard_map/all_to_all | solution.py:75
  67.3 45.5 %reduce-scatter.2.cloned.1.call-start = ((), (), s32[]{:S(2)}) async-start(), calls=%async_computation.3 | async-start | bytes 819200 | tf_op jit(solution)/shard_map/reduce_scatter | solution.py:68
  87.9 27.4 %copy-start.1 = (bf16[1,384,2560]{2,1,0:T(8,128)(2,1)S(1)}, bf16[1,384,2560]{2,1,0:T(8,128)(2,1)}, u32[]{:S(2)}) copy-start(bf16[1,384,2560]{2,1,0:T(8,128)(2,1)} %all-gather.4.cloned.1.call-done) | copy-start | bytes 5898244
  113.8 4.5 %collective-permute-start = (bf16[64,640]{1,0:T(8,128)(2,1)S(1)}, bf16[64,640]{1,0:T(8,128)(2,1)S(1)}, u32[]{:S(2)}, u32[]{:S(2)}) collective-permute-start(bf16[64,640]{1,0:T(8,128)(2,1)S(1)} %convert_element_type.36), channel_id=1, source_target_pairs={{0,16},{16,0},{1,17},{17,1},{2,18},{18,2},{3,19},{19,3},{4,20},{20... | collective-permute-start | bytes 245768 | tf_op jit(solution)/shard_map/ppermute | solution.py:10
Sparse Core Ops, SparseCore 0:
  9.6 35.1 all-gather.3
  88.0 24.8 reduce-scatter.1
where the time goes:
time: 126 us
  local copies, waits for them, and re-layouts  32.2 us (26%)
  waiting for transfers between devices  28.5 us (23%)
  blocking collectives  15.6 us (12%)
  between operations  14.2 us (11%)
  other arithmetic  12.6 us (10%)
  matrix products  11.8 us (9%)
  starting transfers between devices  10.8 us (9%)
    all_gather x1, blocking collectives, on_device(): cotangent_whole = lax.all_gather(cotangent[0], 'tensor', axis=1, tiled=True)  15.6 us
    all_to_all x1, waiting for transfers between devices, on_device(): lax.all_to_all(outgoing.reshape(experts_here, groups, capacity, features)...  14.3 us
    mul x3, local copies, waits for them, and re-layouts, place_rows(): gates[:, :, None] * values[:, None, :].astype(jnp.float32)  8.23 us
    reshape x2, local copies, waits for them, and re-layouts, on_device(): outgoing.reshape(experts_here, groups, capacity, features)  7.22 us
    scatter x1, other arithmetic, place_rows(): return outgoing.at[positions].set(scaled.reshape(-1, values.shape[1]))  6.83 us
    all_to_all x1, waiting for transfers between devices, on_device(): lax.all_to_all(partial_value, 'expert', split_axis=1, concat_axis=1, tile...  6.55 us
    reduce_scatter x1, waiting for transfers between devices, on_device(): lax.psum_scatter(summand, 'tensor', scatter_dimension=1, tiled=True)  5.33 us
    all_to_all x1, starting transfers between devices, on_device(): lax.all_to_all(outgoing.reshape(experts_here, groups, capacity, features)...  4.66 us
  transfers between devices with their start and end apart: 5, of which 4 were waited for; matrix products, arithmetic and copies ran while one was open for 44% of the time, Pallas kernels for 0%

commit v1 on v0

--- a/solution.py
+++ b/solution.py
@@ -2,6 +2,14 @@
 import jax.numpy as jnp
 from jax import lax
 from jax.sharding import PartitionSpec as P
+
+
+def see_outputs_all(u):
+    v_now = tuple((u for _ in range(lax.axis_size("tensor"))))
+    shaped = jnp.stack(v_now)
+    fresh = lax.all_to_all(shaped, "tensor", 0, 0)
+    after = jnp.concatenate(fresh, axis=1)
+    return after
 
 
 def shifted(value, axis, steps):
@@ -68,7 +76,7 @@
     summed = lax.psum_scatter(summand, "tensor", scatter_dimension=1, tiled=True)
     layer_out = summed.astype(jnp.bfloat16)
     handed = shifted(layer_out, "phase", 1)
-    cotangent_whole = lax.all_gather(cotangent[0], "tensor", axis=1, tiled=True)
+    cotangent_whole = see_outputs_all(cotangent[0])
     back_positions = row_positions(backward_routes[0], experts_here, groups, capacity)
     total_rows = experts_here * groups * capacity
     outgoing = place_rows(backward_gates[0], cotangent_whole, back_positions, total_rows)

time: 126 us -> 134 us (1.063)
  blocking collectives: 15.6 us -> 0 us
  waiting for transfers between devices: 28.5 us -> 42 us
  starting transfers between devices: 10.8 us -> 16.4 us
  local copies, waits for them, and re-layouts: 32.2 us -> 36.1 us
    all_gather x1 -> x0, blocking collectives: 15.6 us -> none  [on_device(): cotangent_whole = lax.all_gather(cotangent[0], 'tensor', axis=1, tiled=True)]
    all_to_all x1, waiting for transfers between devices: 6.55 us -> 16.5 us  [on_device(): lax.all_to_all(partial_value, 'expert', split_axis=1, concat_axis=1, tile...]
    all_to_all x0 -> x1, starting transfers between devices: none -> 6.35 us  [see_outputs_all(): fresh = lax.all_to_all(shaped, 'tensor', 0, 0)]
    all_to_all x0 -> x1, waiting for transfers between devices: none -> 4.65 us  [see_outputs_all(): fresh = lax.all_to_all(shaped, 'tensor', 0, 0)]
    another operation x0 -> x2, local copies, waits for them, and re-layouts: none -> 2.68 us  [the longest x1 1.67 us: see_outputs_all(): shaped = jnp.stack(v_now)]
  transfers between devices with their start and end apart: 5 -> 6, of which waited for: 4 -> 5; matrix products, arithmetic and copies ran while one was open for 44% -> 42% of each run, Pallas kernels for 0% -> 0%
where the time goes in v1:
time: 134 us; the launch traced here: 133 us
  waiting for transfers between devices  42 us (31%)
  local copies, waits for them, and re-layouts  36.1 us (27%)
  starting transfers between devices  16.4 us (12%)
  between operations  14.2 us (11%)
  other arithmetic  12.6 us (9%)
  matrix products  11.9 us (9%)
    all_to_all x1, waiting for transfers between devices, on_device(): lax.all_to_all(partial_value, 'expert', split_axis=1, concat_axis=1, tile...  16.5 us
    all_to_all x1, waiting for transfers between devices, on_device(): lax.all_to_all(outgoing.reshape(experts_here, groups, capacity, features)...  14 us
    mul x3, local copies, waits for them, and re-layouts, place_rows(): gates[:, :, None] * values[:, None, :].astype(jnp.float32)  8.35 us
    reshape x2, local copies, waits for them, and re-layouts, on_device(): outgoing.reshape(experts_here, groups, capacity, features)  7.34 us
    scatter x1, other arithmetic, place_rows(): return outgoing.at[positions].set(scaled.reshape(-1, values.shape[1]))  6.88 us
    all_to_all x1, starting transfers between devices, see_outputs_all(): fresh = lax.all_to_all(shaped, 'tensor', 0, 0)  6.35 us
    all_to_all x1, waiting for transfers between devices, see_outputs_all(): fresh = lax.all_to_all(shaped, 'tensor', 0, 0)  4.65 us
    convert_element_type x1, local copies, waits for them, and re-layouts, on_device(): picked.astype(jnp.float32) * fore_gates[:, :, None]  4.61 us
  transfers between devices with their start and end apart: 6, of which 5 were waited for; matrix products, arithmetic and copies ran while one was open for 42% of the time, Pallas kernels for 0%

profile of v1, /device:TPU:0, one launch (start us, length us, event | category | flops | bytes accessed | tf_op | source)
XLA Modules:
  0.0 133.2 jit_solution(13930493637760905565)
XLA Ops:
  7.2 1.7 %stack.3 = bf16[4,64,640]{2,1,0:T(8,128)(2,1)} broadcast(bf16[64,640]{1,0:T(8,128)(2,1)} %bitcast.49), dimensions={1,2} | broadcast | bytes 409600 | tf_op jit(solution)/shard_map/stack | solution.py:9
  8.8 6.3 %all-to-all-start.1 = ((bf16[4,64,640]{2,1,0:T(8,128)(2,1)}), bf16[4,64,640]{2,1,0:T(8,128)(2,1)S(1)}, u32[]{:S(2)}, u32[]{:S(2)}) async-start(bf16[4,64,640]{2,1,0:T(8,128)(2,1)} %stack.3), calls=%async_computation.2 | async-start | bytes 655360 | tf_op jit(solution)/shard_map/all_to_all | solution.py:10
  15.2 0.7 all-gather.3.cloned.1.call-update
  15.9 3.2 %convolution_convert_fusion = bf16[3,4,43,2560]{3,2,1,0:T(8,128)(2,1)S(1)} fusion(bf16[1,3,256,2560]{3,2,1,0:T(8,128)(2,1)} %param.12, bf16[3,4,43,256]{3,1,2,0:T(4,128)(2,1)} %bitcast.46), kind=kOutput, calls=%fused_computation.3 | convolution fusion | flops 677652480 | bytes 6838272 | tf_op jit(solution)/shard_map/egmh,ehd->egmd/dot_general | solution.py:70
  19.1 1.8 %copy.51 = bf16[3,4,43,2560]{3,2,0,1:T(8,128)(2,1)} copy(bf16[3,4,43,2560]{3,2,1,0:T(8,128)(2,1)S(1)} %convolution_convert_fusion) | data formatting | bytes 5283840 | tf_op jit(solution)/shard_map/convert_element_type | solution.py:72
  20.9 4.7 %all-to-all-done.1 = bf16[4,64,640]{2,1,0:T(8,128)(2,1)S(1)} async-done(((bf16[4,64,640]{2,1,0:T(8,128)(2,1)}), bf16[4,64,640]{2,1,0:T(8,128)(2,1)S(1)}, u32[]{:S(2)}, u32[]{:S(2)}) %all-to-all-start.1) | async-done | bytes 327712 | tf_op jit(solution)/shard_map/all_to_all | solution.py:10
  25.5 0.7 copy-done.2
  26.3 3.7 %all-to-all-start = ((bf16[3,4,43,2560]{3,2,0,1:T(8,128)(2,1)}), bf16[3,4,43,2560]{3,2,0,1:T(8,128)(2,1)S(1)}, u32[]{:S(2)}, u32[]{:S(2)}) async-start(bf16[3,4,43,2560]{3,2,0,1:T(8,128)(2,1)} %copy.51), calls=%async_computation | async-start | bytes 5898240 | tf_op jit(solution)/shard_map/all_to_all | solution.py:73
  30.0 0.1 copy.59
  30.1 0.1 copy.60
  30.2 0.1 reduce_window_sum.18
  30.4 0.1 copy.63
  30.5 0.1 reduce_sum.55
  30.6 0.1 copy.64
  30.7 0.1 mul.123
  30.9 0.1 squeeze.23
  31.1 1.0 copy.73
  32.1 3.1 %mul.125 = f32[64,6,2560]{2,1,0:T(8,128)} broadcast(bf16[64,2560]{1,0:T(8,128)(2,1)S(1)} %bitcast.43), dimensions={0,2} | broadcast | bytes 4259840 | tf_op jit(solution)/shard_map/mul | solution.py:37
  35.1 5.2 %mul.126 = f32[384,2560]{1,0:T(8,128)} reshape(f32[64,6,2560]{2,1,0:T(8,128)} %mul.125) | data formatting | bytes 7864320 | tf_op jit(solution)/shard_map/mul | solution.py:37
  40.3 6.9 %scatter_custom_fusion = bf16[516,2560]{1,0:T(8,128)(2,1)} fusion(s32[384]{0:T(512)S(1)} %fusion.29, f32[384,2560]{1,0:T(8,128)} %mul.126, f32[384]{0:T(512)S(1)} %mul.123, bf16[]{:T(256)} %constant.32.clone.1), kind=kCustom, calls=%fused_computation.10 | custom fusion | flops 1966080 | bytes 6576130 | tf_op jit(solution)/shard_map/scatter | solution.py:39
  47.2 3.7 %reshape.227 = bf16[3,4,43,2560]{3,2,1,0:T(8,128)(2,1)} reshape(bf16[516,2560]{1,0:T(8,128)(2,1)} %scatter_custom_fusion) | data formatting | bytes 5283840 | tf_op jit(solution)/shard_map/reshape | solution.py:84
  50.9 3.6 %copy.66 = bf16[3,4,43,2560]{3,2,0,1:T(8,128)(2,1)} copy(bf16[3,4,43,2560]{3,2,1,0:T(8,128)(2,1)} %reshape.227) | data formatting | bytes 5283840 | tf_op jit(solution)/shard_map/reshape | solution.py:84
  54.5 16.5 %all-to-all-done = bf16[3,4,43,2560]{3,2,0,1:T(8,128)(2,1)S(1)} async-done(((bf16[3,4,43,2560]{3,2,0,1:T(8,128)(2,1)}), bf16[3,4,43,2560]{3,2,0,1:T(8,128)(2,1)S(1)}, u32[]{:S(2)}, u32[]{:S(2)}) %all-to-all-start) | async-done | bytes 2641952 | tf_op jit(solution)/shard_map/all_to_all | solution.py:73
  71.0 4.6 %all-to-all-start.2 = ((bf16[3,4,43,2560]{3,2,0,1:T(8,128)(2,1)}), bf16[3,4,43,2560]{3,2,0,1:T(8,128)(2,1)}, u32[]{:S(2)}, u32[]{:S(2)}) async-start(bf16[3,4,43,2560]{3,2,0,1:T(8,128)(2,1)} %copy.66), calls=%async_computation.3 | async-start | bytes 5898240 | tf_op jit(solution)/shard_map/all_to_all | solution.py:83
  75.6 0.2 reduce-scatter.2.cloned.1.call-start
  75.8 0.1 copy.53
  75.9 0.1 copy.54
  76.0 0.1 reduce_window_sum.17
  76.1 0.1 copy.56
  76.2 0.1 copy.57
  76.3 0.1 reduce_sum.51
  76.5 0.1 copy.70
  76.6 0.1 squeeze.22
  76.8 1.9 %copy.52 = bf16[3,4,43,2560]{3,2,1,0:T(8,128)(2,1)} copy(bf16[3,4,43,2560]{3,2,0,1:T(8,128)(2,1)S(1)} %all-to-all-done) | data formatting | bytes 5283840 | tf_op jit(solution)/shard_map/all_to_all | solution.py:73
  78.7 2.4 %reshape.225 = bf16[516,2560]{1,0:T(8,128)(2,1)S(1)} reshape(bf16[3,4,43,2560]{3,2,1,0:T(8,128)(2,1)} %copy.52) | data formatting | bytes 5283840 | tf_op jit(solution)/shard_map/reshape | solution.py:74
  81.1 3.3 %gather_fusion = bf16[384,2560]{1,0:T(8,128)(2,1)} fusion(bf16[516,2560]{1,0:T(8,128)(2,1)S(1)} %reshape.225, s32[1024]{0:T(1024)S(1)} %pad_clamp_fusion), kind=kCustom, calls=%fused_computation | custom fusion | bytes 3933696 | tf_op jit(solution)/shard_map/gather | solution.py:74
  84.4 4.6 %reshape.228 = f32[64,6,2560]{2,1,0:T(8,128)} reshape(bf16[384,2560]{1,0:T(8,128)(2,1)} %gather_fusion) | data formatting | bytes 5898240 | tf_op jit(solution)/shard_map/convert_element_type | solution.py:75
  89.0 4.4 %multiply_reduce_fusion = f32[64,2560]{1,0:T(8,128)S(1)} fusion(f32[64,6,2560]{2,1,0:T(8,128)} %reshape.228, f32[64,6]{1,0:T(8,128)S(1)} %bitcast.47), kind=kLoop, calls=%fused_computation.2 | loop fusion | flops 1802240 | bytes 4589056 | tf_op jit(solution)/shard_map/reduce_sum | solution.py:75
  93.4 2.9 %convolution_add_fusion = f32[64,2560]{1,0:T(8,128)} fusion(f32[64,2560]{1,0:T(8,128)S(1)} %multiply_reduce_fusion, bf16[1,384,2560]{2,1,0:T(8,128)(2,1)} %all-gather.3.cloned.1.call-done, bf16[1,64,384]{2,1,0:T(8,128)(2,1)S(1)} %copy-done), kind=kOutput, calls=%fused_computation.8 | convolution fusion | flops 125992960 | bytes 3325952 | tf_op jit(solution)/shard_map/dot_general | solution.py:63
  96.4 14.0 %all-to-all-done.2 = bf16[3,4,43,2560]{3,2,0,1:T(8,128)(2,1)} async-done(((bf16[3,4,43,2560]{3,2,0,1:T(8,128)(2,1)}), bf16[3,4,43,2560]{3,2,0,1:T(8,128)(2,1)}, u32[]{:S(2)}, u32[]{:S(2)}) %all-to-all-start.2) | async-done | bytes 2641952 | tf_op jit(solution)/shard_map/all_to_all | solution.py:83
  110.4 4.5 %fusion.15 = bf16[1,3,4,43,256]{4,3,2,1,0:T(8,128)(2,1)S(1)} fusion(bf16[1,3,256,2560]{3,2,1,0:T(8,128)(2,1)} %param.12, bf16[3,4,43,2560]{3,2,0,1:T(8,128)(2,1)} %all-to-all-done.2), kind=kOutput, calls=%fused_computation.17 | convolution fusion | flops 676463616 | bytes 6838272 | tf_op jit(solution)/shard_map/egmd,ehd->egmh/dot_general | solution.py:90
  114.9 0.8 copy.68
  115.8 4.5 %reduce-scatter.2.cloned.1.call-done = f32[64,640]{1,0:T(8,128)} async-done(((f32[64,2560]{1,0:T(8,128)}), f32[64,640]{1,0:T(8,128)}) %reduce-scatter.2.cloned.1.call-update) | async-done | bytes 163856 | tf_op jit(solution)/shard_map/reduce_scatter | solution.py:76
  120.3 0.9 convert_element_type.40
  121.2 1.6 %collective-permute-start = (bf16[64,640]{1,0:T(8,128)(2,1)S(1)}, bf16[64,640]{1,0:T(8,128)(2,1)S(1)}, u32[]{:S(2)}, u32[]{:S(2)}) collective-permute-start(bf16[64,640]{1,0:T(8,128)(2,1)S(1)} %convert_element_type.40), channel_id=1, source_target_pairs={{0,16},{16,0},{1,17},{17,1},{2,18},{18,2},{3,19},{19,3},{4,20},{20... | collective-permute-start | bytes 245768 | tf_op jit(solution)/shard_map/ppermute | solution.py:18
  122.8 1.4 %fusion.23 = bf16[1,64,384]{2,1,0:T(8,128)(2,1)} fusion(bf16[64,2560]{1,0:T(8,128)(2,1)S(1)} %bitcast.44, bf16[1,384,2560]{2,1,0:T(8,128)(2,1)S(1)} %copy-done.1), kind=kOutput, calls=%fused_computation.19 | convolution fusion | flops 125853696 | bytes 2342912 | tf_op jit(solution)/shard_map/dot_general | solution.py:93
  124.1 1.6 %collective-permute-done = bf16[64,640]{1,0:T(8,128)(2,1)S(1)} collective-permute-done((bf16[64,640]{1,0:T(8,128)(2,1)S(1)}, bf16[64,640]{1,0:T(8,128)(2,1)S(1)}, u32[]{:S(2)}, u32[]{:S(2)}) %collective-permute-start) | collective-permute-done | bytes 81952 | tf_op jit(solution)/shard_map/ppermute | solution.py:18
  125.7 0.6 copy.87
  (28 shorter events, 0.3 us)
Async XLA Ops:
  7.2 86.3 %copy-start = (bf16[1,64,384]{2,1,0:T(8,128)(2,1)S(1)}, bf16[1,64,384]{2,1,0:T(8,128)(2,1)}, u32[]{:S(2)}) copy-start(bf16[1,64,384]{2,1,0:T(8,128)(2,1)} %param.13) | copy-start | bytes 147460
  8.8 16.7 %all-to-all-start.1 = ((bf16[4,64,640]{2,1,0:T(8,128)(2,1)}), bf16[4,64,640]{2,1,0:T(8,128)(2,1)S(1)}, u32[]{:S(2)}, u32[]{:S(2)}) async-start(bf16[4,64,640]{2,1,0:T(8,128)(2,1)} %stack.3), calls=%async_computation.2 | async-start | bytes 655360 | tf_op jit(solution)/shard_map/all_to_all | solution.py:10
  15.2 78.2 %all-gather.3.cloned.1.call-start = ((), (), s32[]{:S(2)}) async-start(), calls=%async_computation.5 | async-start | bytes 2457600 | tf_op jit(solution)/shard_map/all_gather | solution.py:65
  20.9 9.1 %copy-start.3 = (s32[1,64,6]{1,0,2:T(1,128)S(1)}, s32[1,64,6]{1,0,2:T(1,128)}, u32[]{:S(2)}) copy-start(s32[1,64,6]{1,0,2:T(1,128)} %param.15) | copy-start | bytes 4612
  20.9 9.8 %copy-start.5 = (f32[1,64,6]{1,0,2:T(1,128)S(1)}, f32[1,64,6]{1,0,2:T(1,128)}, u32[]{:S(2)}) copy-start(f32[1,64,6]{1,0,2:T(1,128)} %param.16) | copy-start | bytes 4612
  25.5 0.7 copy-start.2
  26.3 44.7 %all-to-all-start = ((bf16[3,4,43,2560]{3,2,0,1:T(8,128)(2,1)}), bf16[3,4,43,2560]{3,2,0,1:T(8,128)(2,1)S(1)}, u32[]{:S(2)}, u32[]{:S(2)}) async-start(bf16[3,4,43,2560]{3,2,0,1:T(8,128)(2,1)} %copy.51), calls=%async_computation | async-start | bytes 5898240 | tf_op jit(solution)/shard_map/all_to_all | solution.py:73
  54.5 21.3 %copy-start.4 = (s32[1,64,6]{1,0,2:T(1,128)S(1)}, s32[1,64,6]{1,0,2:T(1,128)}, u32[]{:S(2)}) copy-start(s32[1,64,6]{1,0,2:T(1,128)} %param.9) | copy-start | bytes 4612
  54.5 22.0 %copy-start.6 = (f32[1,64,6]{1,0,2:T(1,128)S(1)}, f32[1,64,6]{1,0,2:T(1,128)}, u32[]{:S(2)}) copy-start(f32[1,64,6]{1,0,2:T(1,128)} %param.10) | copy-start | bytes 4612
  71.0 39.5 %all-to-all-start.2 = ((bf16[3,4,43,2560]{3,2,0,1:T(8,128)(2,1)}), bf16[3,4,43,2560]{3,2,0,1:T(8,128)(2,1)}, u32[]{:S(2)}, u32[]{:S(2)}) async-start(bf16[3,4,43,2560]{3,2,0,1:T(8,128)(2,1)} %copy.66), calls=%async_computation.3 | async-start | bytes 5898240 | tf_op jit(solution)/shard_map/all_to_all | solution.py:83
  75.6 44.7 %reduce-scatter.2.cloned.1.call-start = ((), (), s32[]{:S(2)}) async-start(), calls=%async_computation.4 | async-start | bytes 819200 | tf_op jit(solution)/shard_map/reduce_scatter | solution.py:76
  96.4 26.4 %copy-start.1 = (bf16[1,384,2560]{2,1,0:T(8,128)(2,1)S(1)}, bf16[1,384,2560]{2,1,0:T(8,128)(2,1)}, u32[]{:S(2)}) copy-start(bf16[1,384,2560]{2,1,0:T(8,128)(2,1)} %all-gather.3.cloned.1.call-done) | copy-start | bytes 5898244
  121.2 4.5 %collective-permute-start = (bf16[64,640]{1,0:T(8,128)(2,1)S(1)}, bf16[64,640]{1,0:T(8,128)(2,1)S(1)}, u32[]{:S(2)}, u32[]{:S(2)}) collective-permute-start(bf16[64,640]{1,0:T(8,128)(2,1)S(1)} %convert_element_type.40), channel_id=1, source_target_pairs={{0,16},{16,0},{1,17},{17,1},{2,18},{18,2},{3,19},{19,3},{4,20},{20... | collective-permute-start | bytes 245768 | tf_op jit(solution)/shard_map/ppermute | solution.py:18
Sparse Core Ops, SparseCore 0:
  17.6 29.5 all-gather.2
  96.5 23.7 reduce-scatter.1
